TPU v7x, 128 devices: a whole 4x4x4 slice. The times are simulated.
128 devices in a mesh: chan: 8 (over y, core), inp: 16 (over z, x).
Axes of the slice: x: 4, y: 4, z: 4, core: 2. Of those that a mesh axis runs over, the one named last changes fastest.
Arguments:
- voltages: bfloat16 [1024, 262144], P('inp', 'chan'), may hold values from -64 to 64
- tile_table: int32 [144, 2], replicated, may hold values from -1 to 15, as said below
Outputs:
- coherence: float32 [512, 144, 64, 128], P('chan', 'inp')
Inputs may be any that keep to these rules, and one draw needn't show every extreme that they name: `tile_table`: rows 9 d to 9 d + 8 are the slots whose tiles the device at index d along inp outputs. Every pair (a, b) with 0 <= a <= b < 16 stands in exactly one row, and every other row is (-1, -1); the pairs are spread over the rows in any order.
All inputs are finite; a program needn't handle non-finite values.
Results may differ from a plain program's by a relative error of at most 0.0058.
Values may be sent and summed in bfloat16 or wider, within the bound.
No kernel may reach another device: no remote copies, remote signals or barrier semaphores. Data moves between devices by JAX's collectives and lax.ppermute only.
A program may use at most 128 MiB of HBM per device.

v0:
```python
import math
import jax
import jax.numpy as jnp
from jax import lax
from jax.sharding import Mesh
from jax.sharding import PartitionSpec as P

L = 2048
NCH = 512
TAPS = 4
CHAN = ("chan_0", "chan_1")


def passed_along(array, axis, by):
    devices = lax.axis_size(axis)
    pairs = [(i, i + by) for i in range(devices) if 0 <= i + by < devices]
    return lax.ppermute(array, axis, pairs)


def in_blocks(array, dim, devices):
    before, after = (array.shape[:dim], array.shape[dim + 1 :])
    return jnp.moveaxis(array.reshape(*before, devices, -1, *after), dim, 0)


def laid_out(parts, dim):
    parts = jnp.moveaxis(parts, 0, dim)
    shape = parts.shape
    return parts.reshape(*shape[:dim], shape[dim] * shape[dim + 1], *shape[dim + 2 :])


def exchange_in_order(parts, axes, order):
    inside = parts.shape[1:]
    whole = parts.reshape(*(lax.axis_size(a) for a in axes), *inside)
    for k in order:
        whole = lax.all_to_all(whole, axes[k], k, k, tiled=True)
    return whole.reshape(-1, *inside)


def core_and_chips(array, groups, order, split_dim, concat_dim):
    devices = lax.axis_size(groups[0]) * lax.axis_size(groups[1])
    parts = in_blocks(array, split_dim, devices)
    return laid_out(exchange_in_order(parts, groups, order), concat_dim)


def filter_window():
    positions = jnp.arange(TAPS * L, dtype=jnp.float32)
    shape_sinc = jnp.sinc((positions - TAPS * L / 2.0) / L)
    tapering = 0.5 - 0.5 * jnp.cos(2.0 * math.pi * positions / (TAPS * L))
    return (shape_sinc * tapering).reshape(TAPS, L)


def transform_table():
    samples = jnp.arange(L, dtype=jnp.int32)[:, None]
    channels = jnp.arange(NCH, dtype=jnp.int32)[None, :]
    phases = samples * channels % L
    angles = phases.astype(jnp.float32) * (2.0 * math.pi / L)
    return (
        jnp.stack([jnp.cos(angles), -jnp.sin(angles)], axis=2)
        .reshape(L, 2 * NCH)
        .astype(jnp.bfloat16)
    )


def rotate_parts(rows):
    half_width = rows.shape[-1] // 2
    return jnp.concatenate([-rows[..., half_width:], rows[..., :half_width]], axis=-1)


def arrange(turned):
    input_count, frame_total, column_count = turned.shape
    return (
        turned.reshape(input_count, frame_total, column_count // 2, 2)
        .transpose(2, 0, 3, 1)
        .reshape(column_count // 2, input_count, 2 * frame_total)
    )


def channelize(voltages):
    block_width, local_len = voltages.shape
    local_frames = local_len // L
    blocks = voltages.reshape(block_width, local_frames, L)
    following = passed_along(blocks[:, : TAPS - 1, :], CHAN, -1)
    extended = jnp.concatenate([blocks, following], axis=1)
    window = filter_window()
    filtered = jnp.zeros((block_width, local_frames, L), jnp.float32)
    for tap_index in range(TAPS):
        filtered = (
            filtered
            + extended[:, tap_index : tap_index + local_frames, :].astype(jnp.float32)
            * window[tap_index]
        )
    filtered = filtered.astype(jnp.bfloat16).reshape(block_width * local_frames, L)
    spectra = jnp.dot(filtered, transform_table(), preferred_element_type=jnp.float32).astype(
        jnp.bfloat16
    )
    return spectra.reshape(block_width, local_frames, 2 * NCH)


def make_tile(everything, autopower, row_block, col_block, block_width, frame_total):
    present = (row_block >= 0).astype(jnp.float32)
    first = jnp.maximum(row_block, 0)
    second = jnp.maximum(col_block, 0)
    left_rows = lax.dynamic_slice_in_dim(everything, first * block_width, block_width, 1)
    right_rows = lax.dynamic_slice_in_dim(everything, second * block_width, block_width, 1)
    partner = jnp.concatenate([right_rows, rotate_parts(right_rows)], axis=1)
    product = jnp.einsum("cif,cjf->cij", left_rows, partner, preferred_element_type=jnp.float32)
    power_left = lax.dynamic_slice_in_dim(autopower, first * block_width, block_width, 1)
    power_right = lax.dynamic_slice_in_dim(autopower, second * block_width, block_width, 1)
    inverse = present / (frame_total * jnp.sqrt(power_left[:, :, None] * power_right[:, None, :]))
    return product * jnp.concatenate([inverse, inverse], axis=2)


def on_device(voltages, tile_table):
    block_width = voltages.shape[0]
    spectra = channelize(voltages)
    turned = core_and_chips(spectra, ("chan_0", "chan_1"), (1, 0), 2, 1)
    own = arrange(turned)
    everything = lax.all_gather(own, "inp", axis=1, tiled=True)
    frame_total = everything.shape[2] // 2
    autopower = jnp.sum(jnp.square(everything.astype(jnp.float32)), axis=2) / frame_total + 1e-06
    slot_total = tile_table.shape[0] // lax.axis_size("inp")
    device_index = lax.axis_index("inp")
    slot_rows = lax.dynamic_slice_in_dim(tile_table, device_index * slot_total, slot_total, 0)
    outputs = jnp.zeros(
        (everything.shape[0], slot_total, block_width, 2 * block_width), jnp.float32
    )

    def place(slot_index, current):
        tile_out = make_tile(
            everything,
            autopower,
            slot_rows[slot_index, 0],
            slot_rows[slot_index, 1],
            block_width,
            frame_total,
        )
        return lax.dynamic_update_index_in_dim(current, tile_out, slot_index, 1)

    return lax.fori_loop(0, slot_total, place, outputs)


def solution(mesh):
    torus = Mesh(mesh.devices.reshape(4, 2, mesh.shape["inp"]), ("chan_0", "chan_1", "inp"))
    placed = (P("inp", CHAN), P())
    return jax.shard_map(
        on_device,
        mesh=torus,
        in_specs=placed,
        out_specs=P(CHAN, "inp", None, None),
        check_vma=False,
    )
```

profile of v0, /device:TPU:1, one launch (start us, length us, event | category | flops | bytes accessed | tf_op | source)
XLA Modules:
  0.0 443.4 jit_solution(10876512019919204436)
XLA Ops:
  6.5 4.6 %copy.31 = bf16[8,8,16,2048]{3,2,1,0:T(8,128)(2,1)S(1)} copy(bf16[8,8,16,2048]{3,1,2,0:T(8,128)(2,1)} %bitcast.47) | data formatting | bytes 8388608
  14.3 3.5 collective-permute-start
  17.8 17.1 %negate_convert_fusion = (bf16[2048,512,1]{1,0,2:T(8,128)(2,1)S(1)}, bf16[2048,512,1]{1,0,2:T(8,128)(2,1)S(1)}) fusion(), kind=kLoop, calls=%fused_computation.29 | loop fusion | flops 17825792 | bytes 4194304 | tf_op jit(solution)/shard_map/convert.2
  34.9 2.3 pad_maximum_fusion
  37.2 11.3 %copy.21 = bf16[2048,512,2]{0,2,1:T(2,128)(2,1)} copy(bf16[2048,512,2]{1,0,2:T(8,128)(2,1)} %pad_maximum_fusion) | data formatting | bytes 8388608 | tf_op jit(solution)/shard_map/stack | solution.py:58
  48.6 7.3 %convert_element_type.68 = bf16[2048,1024]{0,1:T(8,128)(2,1)} reshape(bf16[2048,512,2]{0,2,1:T(2,128)(2,1)} %copy.21) | data formatting | bytes 8388608 | tf_op jit(solution)/shard_map/convert_element_type | solution.py:60
  56.0 2.7 constant_dynamic-update-slice_fusion
  59.8 5.0 %add_convert_fusion = bf16[64,16,2048]{2,1,0:T(8,128)(2,1)S(1)} fusion(bf16[64,19,2048]{2,1,0:T(8,128)(2,1)S(1)} %copy_dynamic-update-slice_fusion, f32[2048]{0:T(1024)S(1)} %get-tuple-element.117, f32[2048]{0:T(1024)S(1)} %get-tuple-element.118, f32[2048]{0:T(1024)S(1)} %get-tuple-element.119, f32[2048]{0:T(1024)S(1)} %get-tuple-element.116, ...), kind=kLoop, calls=%fused_computation.21 | loop fusion | flops 25165824 | bytes 21004288 | tf_op jit(solution)/shard_map/convert_element_type | solution.py:92
  64.7 4.8 %convert_bitcast_fusion = bf16[128,8,8,128]{3,1,2,0:T(8,128)(2,1)S(1)} fusion(bf16[1024,2048]{1,0:T(8,128)(2,1)S(1)} %bitcast.46, bf16[2048,1024]{0,1:T(8,128)(2,1)S(1)} %copy-done.4), kind=kOutput, calls=%fused_computation.34 | convolution fusion | flops 4296015872 | bytes 10485760 | tf_op jit(solution)/shard_map/dot_general | solution.py:93
  70.8 5.1 %all_to_all.10 = bf16[4,2,64,16,128]{4,3,2,0,1:T(8,128)(2,1)S(1)} all-to-all(bf16[4,2,64,16,128]{4,3,2,0,1:T(8,128)(2,1)S(1)} %copy.23), channel_id=1, replica_groups=mesh['chan_0'=4,'chan_1'=2,'inp'=16] {'chan_1'}, dimensions={1} | all-to-all | bytes 4194304 | tf_op jit(solution)/shard_map/all_to_all | solution.py:35
  76.2 29.6 %all_to_all.11 = bf16[4,2,64,16,128]{4,3,2,1,0:T(8,128)(2,1)S(1)} all-to-all(bf16[4,2,64,16,128]{4,3,2,1,0:T(8,128)(2,1)S(1)} %copy.24), channel_id=1, replica_groups=mesh['chan_0'=4,'chan_1'=2,'inp'=16] {'chan_0'}, dimensions={0} | all-to-all | bytes 4194304 | tf_op jit(solution)/shard_map/all_to_all | solution.py:35
  105.8 7.4 %copy.25 = bf16[8,64,16,128]{1,2,0,3:T(8,128)(2,1)} copy(bf16[8,64,16,128]{3,2,1,0:T(8,128)(2,1)S(1)} %bitcast.43) | data formatting | bytes 4194304 | tf_op jit(solution)/shard_map/reshape | solution.py:36
  113.1 4.8 %copy.26 = bf16[64,64,256]{2,1,0:T(8,128)(2,1)} copy(bf16[64,64,256]{1,2,0:T(8,128)(2,1)} %bitcast.42) | data formatting | bytes 4194304 | tf_op jit(solution)/shard_map/reshape | solution.py:74
  118.0 198.5 %all-gather.2.cloned.1.call-done = bf16[64,1024,256]{2,1,0:T(8,128)(2,1)} async-done(((bf16[64,64,256]{2,1,0:T(8,128)(2,1)}), bf16[64,1024,256]{2,1,0:T(8,128)(2,1)}) %all-gather.2.cloned.1.call-update) | async-done | bytes 33554448 | tf_op jit(solution)/shard_map/all_gather | solution.py:118
  316.5 11.9 %multiply_reduce_fusion = f32[64,1024]{1,0:T(8,128)S(1)} fusion(bf16[64,1024,256]{2,1,0:T(8,128)(2,1)} %all-gather.2.cloned.1.call-done), kind=kLoop, calls=%fused_computation.20 | loop fusion | flops 50266112 | bytes 33816576 | tf_op jit(solution)/shard_map/reduce_sum | solution.py:120
  328.4 107.4 %while.13 = (s32[]{:T(128)}, f32[64,9,64,128]{3,2,1,0:T(8,128)}, s32[9,2]{0,1:T(2,128)S(1)}, bf16[64,1024,256]{2,1,0:T(8,128)(2,1)}, f32[64,1024]{1,0:T(8,128)S(...) while((s32[]{:T(128)}, f32[64,9,64,128]{3,2,1,0:T(8,128)}, ...), condition=%wide.region_2.3_spmd, body=%wide.region_1.2_spmd.sunk | while | flops 284426240 | bytes 18973484 | solution.py:139
  331.9 2.1 dynamic-slice_negate_fusion.2
  335.8 4.6 %fusion.57 = f32[64,9,64,128]{3,2,1,0:T(8,128)} fusion(f32[64,9,64,128]{3,2,1,0:T(8,128)} %get-tuple-element.177, s32[]{:T(128)} %get-tuple-element.176, f32[64,64,64]{2,1,0:T(8,128)S(1)} %multiply_divide_fusion.2, bf16[64,64,128]{2,1,0:T(8,128)(2,1)S(1)} %get-tuple-element.163, bf16[64,64,128]{2,1,0:T(8,128)(2,1)S(1)} %get-tuple-element.164, ...), kind=kOutput, calls=%fused_computation.8.clone.1 | convolution fusion | flops 282066944 | bytes 9437700 | tf_op jit(solution)/shard_map/while/body/eval_jaxpr/cif,cjf->cij/dot_general | solution.py:106
  343.8 2.1 dynamic-slice_negate_fusion.2
  347.7 4.6 %fusion.57 = f32[64,9,64,128]{3,2,1,0:T(8,128)} fusion(f32[64,9,64,128]{3,2,1,0:T(8,128)} %get-tuple-element.177, s32[]{:T(128)} %get-tuple-element.176, f32[64,64,64]{2,1,0:T(8,128)S(1)} %multiply_divide_fusion.2, bf16[64,64,128]{2,1,0:T(8,128)(2,1)S(1)} %get-tuple-element.163, bf16[64,64,128]{2,1,0:T(8,128)(2,1)S(1)} %get-tuple-element.164, ...), kind=kOutput, calls=%fused_computation.8.clone.1 | convolution fusion | flops 282066944 | bytes 9437700 | tf_op jit(solution)/shard_map/while/body/eval_jaxpr/cif,cjf->cij/dot_general | solution.py:106
  355.8 2.1 dynamic-slice_negate_fusion.2
  359.6 4.6 %fusion.57 = f32[64,9,64,128]{3,2,1,0:T(8,128)} fusion(f32[64,9,64,128]{3,2,1,0:T(8,128)} %get-tuple-element.177, s32[]{:T(128)} %get-tuple-element.176, f32[64,64,64]{2,1,0:T(8,128)S(1)} %multiply_divide_fusion.2, bf16[64,64,128]{2,1,0:T(8,128)(2,1)S(1)} %get-tuple-element.163, bf16[64,64,128]{2,1,0:T(8,128)(2,1)S(1)} %get-tuple-element.164, ...), kind=kOutput, calls=%fused_computation.8.clone.1 | convolution fusion | flops 282066944 | bytes 9437700 | tf_op jit(solution)/shard_map/while/body/eval_jaxpr/cif,cjf->cij/dot_general | solution.py:106
  367.7 2.1 dynamic-slice_negate_fusion.2
  371.6 4.6 %fusion.57 = f32[64,9,64,128]{3,2,1,0:T(8,128)} fusion(f32[64,9,64,128]{3,2,1,0:T(8,128)} %get-tuple-element.177, s32[]{:T(128)} %get-tuple-element.176, f32[64,64,64]{2,1,0:T(8,128)S(1)} %multiply_divide_fusion.2, bf16[64,64,128]{2,1,0:T(8,128)(2,1)S(1)} %get-tuple-element.163, bf16[64,64,128]{2,1,0:T(8,128)(2,1)S(1)} %get-tuple-element.164, ...), kind=kOutput, calls=%fused_computation.8.clone.1 | convolution fusion | flops 282066944 | bytes 9437700 | tf_op jit(solution)/shard_map/while/body/eval_jaxpr/cif,cjf->cij/dot_general | solution.py:106
  379.6 2.1 dynamic-slice_negate_fusion.2
  383.5 4.6 %fusion.57 = f32[64,9,64,128]{3,2,1,0:T(8,128)} fusion(f32[64,9,64,128]{3,2,1,0:T(8,128)} %get-tuple-element.177, s32[]{:T(128)} %get-tuple-element.176, f32[64,64,64]{2,1,0:T(8,128)S(1)} %multiply_divide_fusion.2, bf16[64,64,128]{2,1,0:T(8,128)(2,1)S(1)} %get-tuple-element.163, bf16[64,64,128]{2,1,0:T(8,128)(2,1)S(1)} %get-tuple-element.164, ...), kind=kOutput, calls=%fused_computation.8.clone.1 | convolution fusion | flops 282066944 | bytes 9437700 | tf_op jit(solution)/shard_map/while/body/eval_jaxpr/cif,cjf->cij/dot_general | solution.py:106
  391.6 2.1 dynamic-slice_negate_fusion.2
  395.4 4.6 %fusion.57 = f32[64,9,64,128]{3,2,1,0:T(8,128)} fusion(f32[64,9,64,128]{3,2,1,0:T(8,128)} %get-tuple-element.177, s32[]{:T(128)} %get-tuple-element.176, f32[64,64,64]{2,1,0:T(8,128)S(1)} %multiply_divide_fusion.2, bf16[64,64,128]{2,1,0:T(8,128)(2,1)S(1)} %get-tuple-element.163, bf16[64,64,128]{2,1,0:T(8,128)(2,1)S(1)} %get-tuple-element.164, ...), kind=kOutput, calls=%fused_computation.8.clone.1 | convolution fusion | flops 282066944 | bytes 9437700 | tf_op jit(solution)/shard_map/while/body/eval_jaxpr/cif,cjf->cij/dot_general | solution.py:106
  407.4 4.6 %fusion.57 = f32[64,9,64,128]{3,2,1,0:T(8,128)} fusion(f32[64,9,64,128]{3,2,1,0:T(8,128)} %get-tuple-element.177, s32[]{:T(128)} %get-tuple-element.176, f32[64,64,64]{2,1,0:T(8,128)S(1)} %multiply_divide_fusion.2, bf16[64,64,128]{2,1,0:T(8,128)(2,1)S(1)} %get-tuple-element.163, bf16[64,64,128]{2,1,0:T(8,128)(2,1)S(1)} %get-tuple-element.164, ...), kind=kOutput, calls=%fused_computation.8.clone.1 | convolution fusion | flops 282066944 | bytes 9437700 | tf_op jit(solution)/shard_map/while/body/eval_jaxpr/cif,cjf->cij/dot_general | solution.py:106
  419.3 4.6 %fusion.57 = f32[64,9,64,128]{3,2,1,0:T(8,128)} fusion(f32[64,9,64,128]{3,2,1,0:T(8,128)} %get-tuple-element.177, s32[]{:T(128)} %get-tuple-element.176, f32[64,64,64]{2,1,0:T(8,128)S(1)} %multiply_divide_fusion.2, bf16[64,64,128]{2,1,0:T(8,128)(2,1)S(1)} %get-tuple-element.163, bf16[64,64,128]{2,1,0:T(8,128)(2,1)S(1)} %get-tuple-element.164, ...), kind=kOutput, calls=%fused_computation.8.clone.1 | convolution fusion | flops 282066944 | bytes 9437700 | tf_op jit(solution)/shard_map/while/body/eval_jaxpr/cif,cjf->cij/dot_general | solution.py:106
  427.4 2.1 dynamic-slice_negate_fusion.2
  431.2 4.6 %fusion.57 = f32[64,9,64,128]{3,2,1,0:T(8,128)} fusion(f32[64,9,64,128]{3,2,1,0:T(8,128)} %get-tuple-element.177, s32[]{:T(128)} %get-tuple-element.176, f32[64,64,64]{2,1,0:T(8,128)S(1)} %multiply_divide_fusion.2, bf16[64,64,128]{2,1,0:T(8,128)(2,1)S(1)} %get-tuple-element.163, bf16[64,64,128]{2,1,0:T(8,128)(2,1)S(1)} %get-tuple-element.164, ...), kind=kOutput, calls=%fused_computation.8.clone.1 | convolution fusion | flops 282066944 | bytes 9437700 | tf_op jit(solution)/shard_map/while/body/eval_jaxpr/cif,cjf->cij/dot_general | solution.py:106
  (63 shorter events, 40.4 us)
Async XLA Ops:
  6.5 111.4 %copy-start = (s32[144,2]{0,1:T(2,128)S(1)}, s32[144,2]{0,1:T(2,128)}, u32[]{:S(2)}) copy-start(s32[144,2]{0,1:T(2,128)} %param.5) | copy-start | bytes 3460
  6.5 310.0 %all-gather.2.cloned.1.call-start = ((), (), s32[]{:S(2)}) async-start(), calls=%async_computation.2 | async-start | bytes 35651584 | tf_op jit(solution)/shard_map/all_gather | solution.py:118
  11.1 2.0 copy-start.2
  14.3 44.4 %collective-permute-start = (bf16[64,3,2048]{2,0,1:T(8,128)(2,1)S(1)}, bf16[64,3,2048]{2,0,1:T(8,128)(2,1)S(1)}, u32[]{:S(2)}, u32[]{:S(2)}) collective-permute-start(bf16[64,3,2048]{2,0,1:T(8,128)(2,1)S(1)} %copy.19), channel_id=1, source_target_pairs={{16,0},{32,16},{48,32},{64,48},{80,64},{96,80},{112,96},{17,1},{33... | collective-permute-start | bytes 2359304 | tf_op jit(solution)/shard_map/ppermute | solution.py:17
  56.0 3.7 copy-start.3
  59.8 5.0 %copy-start.4 = (bf16[2048,1024]{0,1:T(8,128)(2,1)S(1)}, bf16[2048,1024]{0,1:T(8,128)(2,1)}, u32[]{:S(2)}) copy-start(bf16[2048,1024]{0,1:T(8,128)(2,1)} %convert_element_type.68) | copy-start | bytes 12582916
  435.8 0.7 copy-start.1
Sparse Core Ops, SparseCore 0:
  118.0 198.4 all-gather.1
where the time goes:
time: 445 us; the launch traced here: 443 us
  waiting for transfers between devices  199 us (45%)
  local copies, waits for them, and re-layouts  66.6 us (15%)
  other arithmetic  62.7 us (14%)
  matrix products  46.3 us (10%)
  blocking collectives  34.6 us (8%)
  loops' own time  17.5 us (4%)
  between operations  13.6 us (3%)
    all_gather x1, waiting for transfers between devices, on_device(): everything = lax.all_gather(own, 'inp', axis=1, tiled=True)  198 us
    dot_general x9, matrix products, make_tile(): jnp.einsum('cif,cjf->cij', left_rows, partner, preferred_element_type=jnp...  41.6 us
    all_to_all x2, blocking collectives, exchange_in_order(): whole = lax.all_to_all(whole, axes[k], k, k, tiled=True)  34.6 us
    neg x9, other arithmetic, rotate_parts(): -rows[..., half_width:]  18.8 us
    another operation x1, loops' own time, on_device(): return lax.fori_loop(0, slot_total, place, outputs)  17.5 us
    another operation x1, other arithmetic  17.1 us
    dynamic_slice x9, local copies, waits for them, and re-layouts, make_tile(): lax.dynamic_slice_in_dim(everything, second * block_width, block_width, 1)  15.7 us
    reduce_sum x1, other arithmetic, on_device(): jnp.sum(jnp.square(everything.astype(jnp.float32)), axis=2) / frame_total  11.9 us
  transfers between devices with their start and end apart: 2, of which 1 were waited for; matrix products, arithmetic and copies ran while one was open for 9% of the time, Pallas kernels for 0%

commit v1 on v0

--- a/solution.py
+++ b/solution.py
@@ -115,7 +115,9 @@
     spectra = channelize(voltages)
     turned = core_and_chips(spectra, ("chan_0", "chan_1"), (1, 0), 2, 1)
     own = arrange(turned)
-    everything = lax.all_gather(own, "inp", axis=1, tiled=True)
+    everything = jnp.concatenate(
+        lax.all_to_all(jnp.stack([own] * lax.axis_size("inp")), "inp", 0, 0), axis=1
+    )
     frame_total = everything.shape[2] // 2
     autopower = jnp.sum(jnp.square(everything.astype(jnp.float32)), axis=2) / frame_total + 1e-06
     slot_total = tile_table.shape[0] // lax.axis_size("inp")

time: 445 us -> 769 us (1.73)
  waiting for transfers between devices: 199 us -> 495 us
  local copies, waits for them, and re-layouts: 66.6 us -> 99.5 us
  between operations: 13.6 us -> 0.21 us
    all_to_all x0 -> x1, waiting for transfers between devices: none -> 495 us  [on_device(): lax.all_to_all(jnp.stack([own] * lax.axis_size('inp')), 'inp', 0, 0)]
    all_gather x1 -> x0, waiting for transfers between devices: 198 us -> none  [on_device(): everything = lax.all_gather(own, 'inp', axis=1, tiled=True)]
    all_to_all x0 -> x1, local copies, waits for them, and re-layouts: none -> 22.9 us  [on_device(): lax.all_to_all(jnp.stack([own] * lax.axis_size('inp')), 'inp', 0, 0)]
    another operation x0 -> x2, local copies, waits for them, and re-layouts: none -> 14.7 us  [on_device(): jnp.stack([own] * lax.axis_size('inp'))]
  transfers between devices with their start and end apart: 2 -> 2, of which waited for: 1 -> 1; matrix products, arithmetic and copies ran while one was open for 9% -> 5% of each run, Pallas kernels for 0% -> 0%
where the time goes in v1:
time: 769 us; the launch traced here: 766 us
  waiting for transfers between devices  495 us (64%)
  local copies, waits for them, and re-layouts  99.5 us (13%)
  other arithmetic  62.7 us (8%)
  matrix products  46.4 us (6%)
  blocking collectives  34.6 us (4%)
  loops' own time  16.5 us (2%)
  starting transfers between devices  11.1 us (1%)
    all_to_all x1, waiting for transfers between devices, on_device(): lax.all_to_all(jnp.stack([own] * lax.axis_size('inp')), 'inp', 0, 0)  495 us
    dot_general x9, matrix products, make_tile(): jnp.einsum('cif,cjf->cij', left_rows, partner, preferred_element_type=jnp...  41.6 us
    all_to_all x2, blocking collectives, exchange_in_order(): whole = lax.all_to_all(whole, axes[k], k, k, tiled=True)  34.6 us
    all_to_all x1, local copies, waits for them, and re-layouts, on_device(): lax.all_to_all(jnp.stack([own] * lax.axis_size('inp')), 'inp', 0, 0)  22.9 us
    neg x9, other arithmetic, rotate_parts(): -rows[..., half_width:]  18.8 us
    another operation x1, other arithmetic  17.1 us
    another operation x1, loops' own time, on_device(): return lax.fori_loop(0, slot_total, place, outputs)  16.5 us
    dynamic_slice x9, local copies, waits for them, and re-layouts, make_tile(): lax.dynamic_slice_in_dim(everything, second * block_width, block_width, 1)  15.7 us
  transfers between devices with their start and end apart: 2, of which 1 were waited for; matrix products, arithmetic and copies ran while one was open for 5% of the time, Pallas kernels for 0%

profile of v1, /device:TPU:1, one launch (start us, length us, event | category | flops | bytes accessed | tf_op | source)
XLA Modules:
  0.0 766.0 jit_solution(9282711150781596483)
XLA Ops:
  0.0 4.6 copy.33
  7.7 3.5 collective-permute-start
  11.2 17.1 %negate_convert_fusion = (bf16[2048,512,1]{1,0,2:T(8,128)(2,1)S(1)}, bf16[2048,512,1]{1,0,2:T(8,128)(2,1)S(1)}) fusion(), kind=kLoop, calls=%fused_computation.29 | loop fusion | flops 17825792 | bytes 4194304 | tf_op jit(solution)/shard_map/convert.2
  28.4 2.3 pad_maximum_fusion
  30.7 11.3 %copy.22 = bf16[2048,512,2]{0,2,1:T(2,128)(2,1)} copy(bf16[2048,512,2]{1,0,2:T(8,128)(2,1)} %pad_maximum_fusion) | data formatting | bytes 8388608 | tf_op jit(solution)/shard_map/stack | solution.py:58
  42.0 7.3 convert_element_type.69
  49.5 2.7 constant_dynamic-update-slice_fusion
  53.2 5.0 add_convert_fusion
  58.2 4.8 convert_bitcast_fusion
  64.2 5.1 all_to_all.15
  69.7 29.6 %all_to_all.16 = bf16[4,2,64,16,128]{4,3,2,1,0:T(8,128)(2,1)S(1)} all-to-all(bf16[4,2,64,16,128]{4,3,2,1,0:T(8,128)(2,1)S(1)} %copy.25), channel_id=1, replica_groups=mesh['chan_0'=4,'chan_1'=2,'inp'=16] {'chan_0'}, dimensions={0} | all-to-all | bytes 4194304 | tf_op jit(solution)/shard_map/all_to_all | solution.py:35
  99.2 7.4 copy.26
  106.6 3.5 copy.27
  110.1 11.1 %stack.10 = bf16[16,64,64,256]{3,2,1,0:T(8,128)(2,1)} broadcast(bf16[64,64,256]{2,1,0:T(8,128)(2,1)S(1)} %copy.27), dimensions={1,2,3} | broadcast | bytes 35651584 | tf_op jit(solution)/shard_map/stack | solution.py:119
  121.2 7.6 all-to-all-start.2
  129.0 494.9 %all-to-all-done.2 = bf16[16,64,64,256]{3,2,1,0:T(8,128)(2,1)} async-done(((bf16[16,64,64,256]{3,2,1,0:T(8,128)(2,1)}), bf16[16,64,64,256]{3,2,1,0:T(8,128)(2,1)}, u32[]{:S(2)}, u32[]{:S(2)}) %all-to-all-start.2) | async-done | bytes 33554464 | tf_op jit(solution)/shard_map/all_to_all | solution.py:119
  623.9 11.8 %multiply_reduce_fusion = f32[64,16,64]{2,1,0:T(8,128)S(1)} fusion(bf16[16,64,64,256]{3,2,1,0:T(8,128)(2,1)} %all-to-all-done.2), kind=kLoop, calls=%fused_computation.20 | loop fusion | flops 50266112 | bytes 33816576 | tf_op jit(solution)/shard_map/reduce_sum | solution.py:122
  636.0 22.9 %copy.28 = bf16[16,64,64,256]{3,2,0,1:T(8,128)(2,1)} copy(bf16[16,64,64,256]{3,2,1,0:T(8,128)(2,1)} %all-to-all-done.2) | data formatting | bytes 67108864 | tf_op jit(solution)/shard_map/all_to_all | solution.py:119
  658.9 106.4 %while.13 = (s32[]{:T(128)}, f32[64,9,64,128]{3,2,1,0:T(8,128)}, s32[9,2]{0,1:T(2,128)S(1)}, bf16[64,1024,256]{2,1,0:T(8,128)(2,1)}, f32[64,1024]{1,0:T(8,128)S(...) while((s32[]{:T(128)}, f32[64,9,64,128]{3,2,1,0:T(8,128)}, ...), condition=%wide.region_2.3_spmd, body=%wide.region_1.2_spmd.sunk | while | flops 284426240 | bytes 18973484 | solution.py:141
  662.3 2.1 dynamic-slice_negate_fusion.2
  666.1 4.6 fusion.57
  674.1 2.1 dynamic-slice_negate_fusion.2
  678.0 4.6 fusion.57
  685.9 2.1 dynamic-slice_negate_fusion.2
  689.8 4.6 fusion.57
  697.8 2.1 dynamic-slice_negate_fusion.2
  701.6 4.6 fusion.57
  713.4 4.6 fusion.57
  725.3 4.6 fusion.57
  737.1 4.6 fusion.57
  748.9 4.6 fusion.57
  760.7 4.6 fusion.57
  (65 shorter events, 46.9 us)
Async XLA Ops:
  0.0 128.9 %copy-start = (s32[144,2]{0,1:T(2,128)S(1)}, s32[144,2]{0,1:T(2,128)}, u32[]{:S(2)}) copy-start(s32[144,2]{0,1:T(2,128)} %param.5) | copy-start | bytes 3460
  4.6 2.0 copy-start.2
  7.7 44.4 %collective-permute-start = (bf16[64,3,2048]{2,0,1:T(8,128)(2,1)S(1)}, bf16[64,3,2048]{2,0,1:T(8,128)(2,1)S(1)}, u32[]{:S(2)}, u32[]{:S(2)}) collective-permute-start(bf16[64,3,2048]{2,0,1:T(8,128)(2,1)S(1)} %copy.20), channel_id=1, source_target_pairs={{16,0},{32,16},{48,32},{64,48},{80,64},{96,80},{112,96},{17,1},{33... | collective-permute-start | bytes 2359304 | tf_op jit(solution)/shard_map/ppermute | solution.py:17
  49.5 3.7 copy-start.3
  53.2 5.0 copy-start.4
  121.2 502.7 %all-to-all-start.2 = ((bf16[16,64,64,256]{3,2,1,0:T(8,128)(2,1)}), bf16[16,64,64,256]{3,2,1,0:T(8,128)(2,1)}, u32[]{:S(2)}, u32[]{:S(2)}) async-start(bf16[16,64,64,256]{3,2,1,0:T(8,128)(2,1)} %stack.10), calls=%async_computation.2 | async-start | bytes 67108864 | tf_op jit(solution)/shard_map/all_to_all | solution.py:119
  765.3 0.7 copy-start.1
